TPU v7x, 32 devices: a whole 2x2x4 slice. The times are simulated.
32 devices in a mesh: fsdp: 8 (over z, y), ep: 4 (over x, core).
Axes of the slice: x: 2, y: 2, z: 4, core: 2. Of those that a mesh axis runs over, the one named last changes fastest.
Arguments:
- tokens: bfloat16 [4096, 3072], P(('fsdp', 'ep')), may hold values from -6 to 6
- expert_ids: int32 [4096, 2], P(('fsdp', 'ep')), may hold values from 0 to 3, all different within a row; in each aligned block of 128 rows (0 to 127, 128 to 255, ...) at most 128 rows name the same one
- gates: float32 [4096, 2], P(('fsdp', 'ep')), may hold values from 0.2 to 1
- up_weight: bfloat16 [4, 3072, 768], P('ep', 'fsdp'), may hold values from -0.109375 to 0.109375
- down_weight: bfloat16 [4, 768, 3072], P('ep', 'fsdp'), may hold values from -0.21875 to 0.21875
- cotangent: bfloat16 [4096, 3072], P(('fsdp', 'ep')), may hold values from -6 to 6
Outputs:
- mixed: bfloat16 [4096, 3072], P(('fsdp', 'ep'))
- token_grad: bfloat16 [4096, 3072], P(('fsdp', 'ep'))
- up_grad: bfloat16 [4, 3072, 768], P('ep', 'fsdp')
- down_grad: bfloat16 [4, 768, 3072], P('ep', 'fsdp')
Inputs may be any that keep to these rules, and one draw needn't show every extreme that they name: `expert_ids`: each token names two different experts. Among the tokens of one device (aligned blocks of 128 tokens) no expert is named more than 128 times, and in some block one expert is named exactly 128 times.
All inputs are finite; a program needn't handle non-finite values.
Results may differ from a plain program's by a relative error of at most 0.012.
Values may be sent and summed in bfloat16 or wider, within the bound.
A program may use at most 128 MiB of HBM per device.

v0:
```python
import jax
import jax.numpy as jnp
from jax import lax
from jax.sharding import PartitionSpec as P


def gelu_parts(pre):
    root = 0.7978845608028654
    inner = root * (pre + 0.044715 * pre * pre * pre)
    tanh_val = jnp.tanh(inner)
    value = 0.5 * pre * (1.0 + tanh_val)
    slope = 0.5 * (1.0 + tanh_val) + 0.5 * pre * (1.0 - tanh_val * tanh_val) * root * (
        1.0 + 3.0 * 0.044715 * pre * pre
    )
    return (value, slope)


def contract_last(left, right):
    return lax.dot_general(
        left, right, (((1,), (1,)), ((), ())), preferred_element_type=jnp.float32
    )


def contract_first(left, right):
    return lax.dot_general(
        left, right, (((0,), (0,)), ((), ())), preferred_element_type=jnp.float32
    )


def body(tokens, expert_ids, gates, up_weight, down_weight, cotangent):
    n_ep = lax.axis_size("ep")
    f32 = jnp.float32
    bf16 = jnp.bfloat16
    chosen = expert_ids[:, :, None] == jnp.arange(n_ep, dtype=jnp.int32)[None, None, :]
    dense_gates = jnp.sum(jnp.where(chosen, gates[:, :, None], 0.0), axis=1)
    all_gates = lax.all_gather(dense_gates, "ep", axis=0, tiled=True)
    mine = lax.axis_index("ep") == jnp.arange(n_ep, dtype=jnp.int32)
    gate = jnp.sum(jnp.where(mine[None, :], all_gates, 0.0), axis=1, keepdims=True)
    rows = lax.all_gather(tokens, "ep", axis=0, tiled=True)
    up = lax.all_gather(up_weight, "fsdp", axis=1, tiled=True)[0]
    cot = lax.all_gather(cotangent, "ep", axis=0, tiled=True)
    down = lax.all_gather(down_weight, "fsdp", axis=1, tiled=True)[0]
    grad_rows = (cot.astype(f32) * gate).astype(bf16)
    pre = jnp.dot(rows, up, preferred_element_type=f32)
    value, slope = gelu_parts(pre)
    hidden = value.astype(bf16)
    down_grad = lax.psum_scatter(
        contract_first(hidden, grad_rows).astype(bf16), "fsdp", scatter_dimension=0, tiled=True
    )
    d_hidden = contract_last(grad_rows, down)
    d_pre = (d_hidden * slope).astype(bf16)
    up_grad = lax.psum_scatter(
        contract_first(rows, d_pre).astype(bf16), "fsdp", scatter_dimension=0, tiled=True
    )
    result = jnp.dot(hidden, down, preferred_element_type=f32)
    mixed = lax.psum_scatter((result * gate).astype(bf16), "ep", scatter_dimension=0, tiled=True)
    back = contract_last(d_pre, up).astype(bf16)
    token_grad = lax.psum_scatter(back, "ep", scatter_dimension=0, tiled=True)
    return (mixed, token_grad, up_grad[None], down_grad[None])


def solution(mesh):
    placed = (
        P(("fsdp", "ep"), None),
        P(("fsdp", "ep"), None),
        P(("fsdp", "ep"), None),
        P("ep", "fsdp", None),
        P("ep", "fsdp", None),
        P(("fsdp", "ep"), None),
    )
    return jax.shard_map(
        body,
        mesh=mesh,
        in_specs=placed,
        out_specs=(
            P(("fsdp", "ep"), None),
            P(("fsdp", "ep"), None),
            P("ep", "fsdp", None),
            P("ep", "fsdp", None),
        ),
        check_vma=False,
    )
```

profile of v0, /device:TPU:0, one launch (start us, length us, event | category | flops | bytes accessed | tf_op | source)
XLA Modules:
  0.0 534.1 jit_solution(15591842795536665031)
XLA Ops:
  7.2 0.7 all-gather.5.cloned.1.call-update
  7.9 0.0 all-gather.7.cloned.1.call-start
  8.0 0.7 all-gather.7.cloned.1.call-update
  8.7 0.7 all-gather.11.cloned.1.call-update
  9.5 0.5 all-gather.9.cloned.1.call-update
  10.0 0.0 reduce-scatter.13.cloned.1.call-start
  10.1 6.1 %all_gather.18 = f32[512,4]{0,1:T(4,128)S(1)} all-gather(f32[128,4]{0,1:T(4,128)S(1)} %select_reduce_fusion.1), channel_id=1, replica_groups=mesh['fsdp'=8,'ep'=4] {'ep'}, dimensions={0}, use_global_device_ids=true | all-gather | bytes 10240 | tf_op jit(solution)/shard_map/all_gather | solution.py:36
  16.2 0.1 select_reduce_fusion
  16.3 24.6 %all-gather.5.cloned.1.call-done = bf16[512,3072]{1,0:T(8,128)(2,1)} async-done(((bf16[128,3072]{1,0:T(8,128)(2,1)}), bf16[512,3072]{1,0:T(8,128)(2,1)}) %all-gather.5.cloned.1.call-update) | async-done | bytes 3145744 | tf_op jit(solution)/shard_map/all_gather | solution.py:39
  40.8 82.1 %all-gather.7.cloned.1.call-done = bf16[1,3072,768]{2,1,0:T(8,128)(2,1)} async-done(((bf16[1,384,768]{2,1,0:T(8,128)(2,1)}), bf16[1,3072,768]{2,1,0:T(8,128)(2,1)}) %all-gather.7.cloned.1.call-update) | async-done | bytes 4718608 | tf_op jit(solution)/shard_map/all_gather | solution.py:40
  122.9 7.1 %fusion.5 = f32[512,768]{1,0:T(8,128)} fusion(bf16[512,3072]{1,0:T(8,128)(2,1)} %all-gather.5.cloned.1.call-done, bf16[1,3072,768]{2,1,0:T(8,128)(2,1)} %all-gather.7.cloned.1.call-done), kind=kOutput, calls=%fused_computation.9 | convolution fusion | flops 2415919104 | bytes 9437184 | tf_op jit(solution)/shard_map/dot_general | solution.py:44
  130.0 21.2 %all-gather.11.cloned.1.call-done = bf16[512,3072]{1,0:T(8,128)(2,1)} async-done(((bf16[128,3072]{1,0:T(8,128)(2,1)}), bf16[512,3072]{1,0:T(8,128)(2,1)}) %all-gather.11.cloned.1.call-update) | async-done | bytes 3145744 | tf_op jit(solution)/shard_map/all_gather | solution.py:41
  151.2 82.0 %all-gather.9.cloned.1.call-done = bf16[1,768,3072]{2,1,0:T(8,128)(2,1)} async-done(((bf16[1,96,3072]{2,1,0:T(8,128)(2,1)}), bf16[1,768,3072]{2,1,0:T(8,128)(2,1)}) %all-gather.9.cloned.1.call-update) | async-done | bytes 4718608 | tf_op jit(solution)/shard_map/all_gather | solution.py:42
  233.2 7.0 %fusion.17 = bf16[512,768]{1,0:T(8,128)(2,1)S(1)} fusion(f32[512,768]{1,0:T(8,128)} %fusion.5, bf16[1,768,3072]{2,1,0:T(8,128)(2,1)} %all-gather.9.cloned.1.call-done, bf16[512,3072]{1,0:T(8,128)(2,1)} %all-gather.11.cloned.1.call-done, f32[512]{0:T(512)S(1)} %select_reduce_fusion), kind=kOutput, calls=%fused_computation.21 | convolution fusion | flops 2428108800 | bytes 10225664 | tf_op jit(solution)/shard_map/dot_general | solution.py:19
  240.2 0.9 copy-done.5
  241.1 4.3 fusion.7
  245.4 6.7 %copy.17 = bf16[3072,768]{1,0:T(8,128)(2,1)} copy(bf16[3072,768]{0,1:T(8,128)(2,1)} %fusion.7) | data formatting | bytes 9437184
  252.2 0.0 reduce-scatter.7.cloned.1.call-start
  252.2 1.3 copy-done.4
  253.6 6.5 %multiply_convert_fusion.1 = bf16[512,3072]{1,0:T(8,128)(2,1)} fusion(bf16[1,768,3072]{2,1,0:T(8,128)(2,1)} %all-gather.9.cloned.1.call-done, f32[512]{0:T(512)S(1)} %select_reduce_fusion, f32[512,768]{1,0:T(8,128)S(1)} %copy-done.4), kind=kOutput, calls=%fused_computation.1 | convolution fusion | flops 2422603776 | bytes 9439232 | tf_op jit(solution)/shard_map/dot_general | solution.py:55
  260.0 0.0 reduce-scatter.9.cloned.1.call-start
  260.1 1.1 copy-done.6
  261.1 6.4 %fusion.8 = bf16[512,3072]{1,0:T(8,128)(2,1)} fusion(bf16[512,768]{1,0:T(8,128)(2,1)S(1)} %copy-done.6, bf16[1,3072,768]{2,1,0:T(8,128)(2,1)} %all-gather.7.cloned.1.call-done), kind=kOutput, calls=%fused_computation.12 | convolution fusion | flops 2417491968 | bytes 8650752 | tf_op jit(solution)/shard_map/dot_general | solution.py:19
  267.6 0.0 reduce-scatter.11.cloned.1.call-start
  267.6 1.8 copy-done.2
  269.5 6.5 %convolution_convert_fusion = bf16[768,3072]{1,0:T(8,128)(2,1)} fusion(bf16[512,3072]{1,0:T(8,128)(2,1)S(1)} %copy-done.2, f32[512]{0:T(512)S(1)} %select_reduce_fusion, f32[512,768]{1,0:T(8,128)} %fusion.5), kind=kOutput, calls=%fused_computation.2 | convolution fusion | flops 2426535936 | bytes 9439232 | tf_op jit(solution)/shard_map/dot_general | solution.py:25
  276.0 69.8 %reduce-scatter.13.cloned.1.call-done = bf16[384,768]{1,0:T(8,128)(2,1)} async-done(((bf16[3072,768]{1,0:T(8,128)(2,1)}), bf16[384,768]{1,0:T(8,128)(2,1)}) %reduce-scatter.13.cloned.1.call-update) | async-done | bytes 589840
  345.7 1.4 copy.18
  347.1 1.1 copy.16
  348.2 38.3 %reduce-scatter.7.cloned.1.call-done = bf16[128,3072]{1,0:T(8,128)(2,1)} async-done(((bf16[512,3072]{1,0:T(8,128)(2,1)}), bf16[128,3072]{1,0:T(8,128)(2,1)}) %reduce-scatter.7.cloned.1.call-update) | async-done | bytes 786448 | tf_op jit(solution)/shard_map/reduce_scatter | solution.py:56
  386.4 41.2 %reduce-scatter.9.cloned.1.call-done = bf16[128,3072]{1,0:T(8,128)(2,1)} async-done(((bf16[512,3072]{1,0:T(8,128)(2,1)}), bf16[128,3072]{1,0:T(8,128)(2,1)}) %reduce-scatter.9.cloned.1.call-update) | async-done | bytes 786448 | tf_op jit(solution)/shard_map/reduce_scatter | solution.py:58
  427.6 99.7 %reduce-scatter.11.cloned.1.call-done = bf16[96,3072]{1,0:T(8,128)(2,1)} async-done(((bf16[768,3072]{1,0:T(8,128)(2,1)}), bf16[96,3072]{1,0:T(8,128)(2,1)}) %reduce-scatter.11.cloned.1.call-update) | async-done | bytes 589840 | tf_op jit(solution)/shard_map/reduce_scatter | solution.py:47
  (19 shorter events, 0.2 us)
Async XLA Ops:
  7.2 2.9 copy-start
  7.2 2.9 copy-start.1
  7.2 33.7 %all-gather.5.cloned.1.call-start = ((), (), s32[]{:S(2)}) async-start(), calls=%async_computation.4 | async-start | bytes 3932160 | tf_op jit(solution)/shard_map/all_gather | solution.py:39
  7.9 115.0 %all-gather.7.cloned.1.call-start = ((), (), s32[]{:S(2)}) async-start(), calls=%async_computation.5 | async-start | bytes 5308416 | tf_op jit(solution)/shard_map/all_gather | solution.py:40
  8.7 142.5 %all-gather.11.cloned.1.call-start = ((), (), s32[]{:S(2)}) async-start(), calls=%async_computation.8 | async-start | bytes 3932160 | tf_op jit(solution)/shard_map/all_gather | solution.py:41
  9.4 223.8 %all-gather.9.cloned.1.call-start = ((), (), s32[]{:S(2)}) async-start(), calls=%async_computation.6 | async-start | bytes 5308416 | tf_op jit(solution)/shard_map/all_gather | solution.py:42
  10.0 335.7 %reduce-scatter.13.cloned.1.call-start = ((), (), s32[]{:S(2)}) async-start(), calls=%async_computation.11 | async-start | bytes 5308416
  130.0 111.0 %copy-start.3 = (bf16[512,3072]{1,0:T(8,128)(2,1)S(1)}, bf16[512,3072]{1,0:T(8,128)(2,1)}, u32[]{:S(2)}) copy-start(bf16[512,3072]{1,0:T(8,128)(2,1)} %all-gather.5.cloned.1.call-done) | copy-start | bytes 9437188
  240.2 0.9 copy-start.5
  252.1 1.4 copy-start.4
  252.2 134.2 %reduce-scatter.7.cloned.1.call-start = ((), (), s32[]{:S(2)}) async-start(), calls=%async_computation.7 | async-start | bytes 3932160 | tf_op jit(solution)/shard_map/reduce_scatter | solution.py:56
  260.0 1.1 copy-start.6
  260.0 167.6 %reduce-scatter.9.cloned.1.call-start = ((), (), s32[]{:S(2)}) async-start(), calls=%async_computation.9 | async-start | bytes 3932160 | tf_op jit(solution)/shard_map/reduce_scatter | solution.py:58
  267.5 1.9 copy-start.2
  267.6 259.7 %reduce-scatter.11.cloned.1.call-start = ((), (), s32[]{:S(2)}) async-start(), calls=%async_computation.10 | async-start | bytes 5308416 | tf_op jit(solution)/shard_map/reduce_scatter | solution.py:47
Sparse Core Ops, SparseCore 0:
  9.6 31.2 all-gather.4
  43.0 79.8 all-gather.6
  124.5 26.6 all-gather.10
  153.3 79.8 all-gather.8
  252.3 93.3 reduce-scatter.12
  348.7 37.6 reduce-scatter.6
  389.7 37.9 reduce-scatter.8
  431.9 95.3 reduce-scatter.10
where the time goes:
time: 535 us; the launch traced here: 534 us
  waiting for transfers between devices  461 us (86%)
  matrix products  37.8 us (7%)
  local copies, waits for them, and re-layouts  14.3 us (3%)
  between operations  14.2 us (3%)
  blocking collectives  6.11 us (1%)
    reduce_scatter x1, waiting for transfers between devices, body(): lax.psum_scatter(contract_first(hidden, grad_rows).astype(bf16), 'fsdp',...  99.7 us
    all_gather x1, waiting for transfers between devices, body(): up = lax.all_gather(up_weight, 'fsdp', axis=1, tiled=True)[0]  82.1 us
    all_gather x1, waiting for transfers between devices, body(): down = lax.all_gather(down_weight, 'fsdp', axis=1, tiled=True)[0]  82 us
    unnamed x9, waiting for transfers between devices  72.4 us
    reduce_scatter x1, waiting for transfers between devices, body(): token_grad = lax.psum_scatter(back, 'ep', scatter_dimension=0, tiled=True)  41.2 us
    reduce_scatter x1, waiting for transfers between devices, body(): lax.psum_scatter((result * gate).astype(bf16), 'ep', scatter_dimension=0,...  38.3 us
    all_gather x1, waiting for transfers between devices, body(): rows = lax.all_gather(tokens, 'ep', axis=0, tiled=True)  24.6 us
    all_gather x1, waiting for transfers between devices, body(): cot = lax.all_gather(cotangent, 'ep', axis=0, tiled=True)  21.2 us
  transfers between devices with their start and end apart: 8, of which 8 were waited for; matrix products, arithmetic and copies ran while one was open for 5% of the time, Pallas kernels for 0%

commit v1 on v0

--- a/solution.py
+++ b/solution.py
@@ -36,7 +36,12 @@
     all_gates = lax.all_gather(dense_gates, "ep", axis=0, tiled=True)
     mine = lax.axis_index("ep") == jnp.arange(n_ep, dtype=jnp.int32)
     gate = jnp.sum(jnp.where(mine[None, :], all_gates, 0.0), axis=1, keepdims=True)
-    rows = lax.all_gather(tokens, "ep", axis=0, tiled=True)
+    ring = [tokens]
+    for hop in range(3):
+        ring.append(lax.ppermute(ring[-1], "ep", [(dev, (dev + 1) % 4) for dev in range(4)]))
+    rows = jnp.roll(
+        jnp.concatenate(ring[::-1], axis=0), (lax.axis_index("ep") + 1) * ring[0].shape[0], axis=0
+    )
     up = lax.all_gather(up_weight, "fsdp", axis=1, tiled=True)[0]
     cot = lax.all_gather(cotangent, "ep", axis=0, tiled=True)
     down = lax.all_gather(down_weight, "fsdp", axis=1, tiled=True)[0]

time: 535 us -> 489 us (0.914)
  waiting for transfers between devices: 461 us -> 415 us
  local copies, waits for them, and re-layouts: 14.3 us -> 7.56 us
  blocking collectives: 6.11 us -> 11.5 us
    reduce_scatter x0 -> x1, waiting for transfers between devices: none -> 99.5 us  [body(): lax.psum_scatter(contract_first(rows, d_pre).astype(bf16), 'fsdp', scatte...]
    unnamed x9 -> x7, waiting for transfers between devices: 72.4 us -> 1.46 us
    all_gather x1, waiting for transfers between devices: 82.1 us -> 40.4 us  [body(): up = lax.all_gather(up_weight, 'fsdp', axis=1, tiled=True)[0]]
    reduce_scatter x1, waiting for transfers between devices: 38.3 us -> 13.5 us  [body(): lax.psum_scatter((result * gate).astype(bf16), 'ep', scatter_dimension=0,...]
    all_gather x1 -> x0, waiting for transfers between devices: 24.6 us -> none  [body(): rows = lax.all_gather(tokens, 'ep', axis=0, tiled=True)]
    ppermute x0 -> x3, waiting for transfers between devices: none -> 23.2 us  [body(): lax.ppermute(ring[-1], 'ep', [(dev, (dev + 1) % 4) for dev in range(4)])]
    unnamed x17 -> x9, local copies, waits for them, and re-layouts: 14.3 us -> 6.61 us
    all_gather x1, waiting for transfers between devices: 82 us -> 74.3 us  [body(): down = lax.all_gather(down_weight, 'fsdp', axis=1, tiled=True)[0]]
  transfers between devices with their start and end apart: 8 -> 10, of which waited for: 8 -> 9; matrix products, arithmetic and copies ran while one was open for 5% -> 10% of each run, Pallas kernels for 0% -> 0%
where the time goes in v1:
time: 489 us
  waiting for transfers between devices  415 us (85%)
  matrix products  39.6 us (8%)
  between operations  14.2 us (3%)
  blocking collectives  11.5 us (2%)
  local copies, waits for them, and re-layouts  7.56 us (2%)
    reduce_scatter x1, waiting for transfers between devices, body(): lax.psum_scatter(contract_first(rows, d_pre).astype(bf16), 'fsdp', scatte...  99.5 us
    reduce_scatter x1, waiting for transfers between devices, body(): lax.psum_scatter(contract_first(hidden, grad_rows).astype(bf16), 'fsdp',...  99.3 us
    all_gather x1, waiting for transfers between devices, body(): down = lax.all_gather(down_weight, 'fsdp', axis=1, tiled=True)[0]  74.3 us
    reduce_scatter x1, waiting for transfers between devices, body(): token_grad = lax.psum_scatter(back, 'ep', scatter_dimension=0, tiled=True)  41.1 us
    all_gather x1, waiting for transfers between devices, body(): up = lax.all_gather(up_weight, 'fsdp', axis=1, tiled=True)[0]  40.4 us
    ppermute x3, waiting for transfers between devices, body(): lax.ppermute(ring[-1], 'ep', [(dev, (dev + 1) % 4) for dev in range(4)])  23.2 us
    all_gather x1, waiting for transfers between devices, body(): cot = lax.all_gather(cotangent, 'ep', axis=0, tiled=True)  21.7 us
    dot_general x2, matrix products, contract_first(): lax.dot_general(left, right, (((0,), (0,)), ((), ())), preferred_element_...  13.8 us
  transfers between devices with their start and end apart: 10, of which 9 were waited for; matrix products, arithmetic and copies ran while one was open for 10% of the time, Pallas kernels for 0%

profile of v1, /device:TPU:0, one launch (start us, length us, event | category | flops | bytes accessed | tf_op | source)
XLA Modules:
  0.0 489.0 jit_solution(6418308995381881234)
XLA Ops:
  7.2 0.7 all-gather.4.cloned.1.call-update
  8.0 0.7 all-gather.6.cloned.1.call-update
  8.7 0.5 collective-permute-start
  9.2 11.8 %collective-permute-done = bf16[128,3072]{1,0:T(8,128)(2,1)S(1)} collective-permute-done((bf16[128,3072]{1,0:T(8,128)(2,1)}, bf16[128,3072]{1,0:T(8,128)(2,1)S(1)}, u32[]{:S(2)}, u32[]{:S(2)}) %collective-permute-start) | collective-permute-done | bytes 786464 | tf_op jit(solution)/shard_map/ppermute | solution.py:41
  21.0 0.0 collective-permute-start.1
  21.1 11.4 %collective-permute-done.1 = bf16[128,3072]{1,0:T(8,128)(2,1)S(1)} collective-permute-done((bf16[128,3072]{1,0:T(8,128)(2,1)S(1)}, bf16[128,3072]{1,0:T(8,128)(2,1)S(1)}, u32[]{:S(2)}, u32[]{:S(2)}) %collective-permute-start.1) | collective-permute-done | bytes 786464 | tf_op jit(solution)/shard_map/ppermute | solution.py:41
  32.5 0.0 reduce-scatter.5.cloned.1.call-start
  32.5 0.7 select_reduce_fusion.1
  33.2 11.5 %all_gather.14 = f32[512,4]{0,1:T(4,128)S(1)} all-gather(f32[128,4]{0,1:T(4,128)S(1)} %select_reduce_fusion.1), channel_id=1, replica_groups=mesh['fsdp'=8,'ep'=4] {'ep'}, dimensions={0}, use_global_device_ids=true | all-gather | bytes 10240 | tf_op jit(solution)/shard_map/all_gather | solution.py:36
  44.7 0.1 select_reduce_fusion
  44.8 0.9 constant_dynamic-update-slice_fusion.7
  45.8 1.0 constant_dynamic-update-slice_fusion.6
  46.7 0.9 constant_dynamic-update-slice_fusion.5
  47.7 0.9 constant_dynamic-update-slice_fusion.4
  48.6 0.9 constant_dynamic-update-slice_fusion.3
  49.5 0.9 constant_dynamic-update-slice_fusion.2
  50.5 1.0 constant_dynamic-update-slice_fusion.1
  51.4 0.9 constant_dynamic-update-slice_fusion
  52.4 40.4 %all-gather.4.cloned.1.call-done = bf16[1,3072,768]{2,1,0:T(8,128)(2,1)} async-done(((bf16[1,384,768]{2,1,0:T(8,128)(2,1)}), bf16[1,3072,768]{2,1,0:T(8,128)(2,1)}) %all-gather.4.cloned.1.call-update) | async-done | bytes 4718608 | tf_op jit(solution)/shard_map/all_gather | solution.py:45
  92.8 5.9 %fusion.5 = f32[512,768]{1,0:T(8,128)S(1)} fusion(bf16[1,3072,768]{2,1,0:T(8,128)(2,1)} %all-gather.4.cloned.1.call-done, bf16[1024,3072]{1,0:T(8,128)(2,1)} %constant_dynamic-update-slice_fusion, s32[]{:T(128)S(6)} %select_n.22), kind=kOutput, calls=%fused_computation.9 | convolution fusion | flops 2415919104 | bytes 9437188 | tf_op jit(solution)/shard_map/dot_general | solution.py:49
  98.7 74.3 %all-gather.6.cloned.1.call-done = bf16[1,768,3072]{2,1,0:T(8,128)(2,1)} async-done(((bf16[1,96,3072]{2,1,0:T(8,128)(2,1)}), bf16[1,768,3072]{2,1,0:T(8,128)(2,1)}) %all-gather.6.cloned.1.call-update) | async-done | bytes 4718608 | tf_op jit(solution)/shard_map/all_gather | solution.py:47
  173.0 6.5 %multiply_convert_fusion.1 = bf16[512,3072]{1,0:T(8,128)(2,1)} fusion(bf16[1,768,3072]{2,1,0:T(8,128)(2,1)} %all-gather.6.cloned.1.call-done, f32[512]{0:T(512)S(1)} %select_reduce_fusion, f32[512,768]{1,0:T(8,128)S(1)} %fusion.5), kind=kOutput, calls=%fused_computation.1 | convolution fusion | flops 2422603776 | bytes 9439232 | tf_op jit(solution)/shard_map/dot_general | solution.py:60
  179.6 21.7 %all-gather.8.cloned.1.call-done = bf16[512,3072]{1,0:T(8,128)(2,1)} async-done(((bf16[128,3072]{1,0:T(8,128)(2,1)}), bf16[512,3072]{1,0:T(8,128)(2,1)}) %all-gather.8.cloned.1.call-update) | async-done | bytes 3145744 | tf_op jit(solution)/shard_map/all_gather | solution.py:46
  201.3 6.6 %fusion.18 = bf16[512,768]{1,0:T(8,128)(2,1)S(1)} fusion(f32[512,768]{1,0:T(8,128)S(1)} %fusion.5, bf16[1,768,3072]{2,1,0:T(8,128)(2,1)} %all-gather.6.cloned.1.call-done, bf16[512,3072]{1,0:T(8,128)(2,1)} %all-gather.8.cloned.1.call-done, f32[512]{0:T(512)S(1)} %select_reduce_fusion), kind=kOutput, calls=%fused_computation.22 | convolution fusion | flops 2428108800 | bytes 10225664 | tf_op jit(solution)/shard_map/dot_general | solution.py:19
  207.9 6.9 %fusion.7 = bf16[512,3072]{1,0:T(8,128)(2,1)} fusion(bf16[512,768]{1,0:T(8,128)(2,1)S(1)} %fusion.18, bf16[1,3072,768]{2,1,0:T(8,128)(2,1)} %all-gather.4.cloned.1.call-done), kind=kOutput, calls=%fused_computation.11 | convolution fusion | flops 2417491968 | bytes 8650752 | tf_op jit(solution)/shard_map/dot_general | solution.py:19
  214.8 0.0 reduce-scatter.9.cloned.1.call-start
  214.9 6.8 %convolution_convert_fusion.1 = bf16[3072,768]{1,0:T(8,128)(2,1)} fusion(bf16[512,768]{1,0:T(8,128)(2,1)S(1)} %fusion.18, bf16[1024,3072]{1,0:T(8,128)(2,1)} %constant_dynamic-update-slice_fusion, s32[]{:T(128)S(6)} %select_n.22), kind=kOutput, calls=%fused_computation.3 | convolution fusion | flops 2418278400 | bytes 8650756 | tf_op jit(solution)/shard_map/dot_general | solution.py:25
  221.7 7.0 %convolution_convert_fusion = bf16[768,3072]{1,0:T(8,128)(2,1)} fusion(bf16[512,3072]{1,0:T(8,128)(2,1)} %all-gather.8.cloned.1.call-done, f32[512]{0:T(512)S(1)} %select_reduce_fusion, f32[512,768]{1,0:T(8,128)S(1)} %fusion.5), kind=kOutput, calls=%fused_computation.2 | convolution fusion | flops 2426535936 | bytes 9439232 | tf_op jit(solution)/shard_map/dot_general | solution.py:25
  228.7 13.5 %reduce-scatter.5.cloned.1.call-done = bf16[128,3072]{1,0:T(8,128)(2,1)} async-done(((bf16[512,3072]{1,0:T(8,128)(2,1)}), bf16[128,3072]{1,0:T(8,128)(2,1)}) %reduce-scatter.5.cloned.1.call-update) | async-done | bytes 786448 | tf_op jit(solution)/shard_map/reduce_scatter | solution.py:61
  242.3 41.1 %reduce-scatter.7.cloned.1.call-done = bf16[128,3072]{1,0:T(8,128)(2,1)} async-done(((bf16[512,3072]{1,0:T(8,128)(2,1)}), bf16[128,3072]{1,0:T(8,128)(2,1)}) %reduce-scatter.7.cloned.1.call-update) | async-done | bytes 786448 | tf_op jit(solution)/shard_map/reduce_scatter | solution.py:63
  283.4 99.5 %reduce-scatter.9.cloned.1.call-done = bf16[384,768]{1,0:T(8,128)(2,1)} async-done(((bf16[3072,768]{1,0:T(8,128)(2,1)}), bf16[384,768]{1,0:T(8,128)(2,1)}) %reduce-scatter.9.cloned.1.call-update) | async-done | bytes 589840 | tf_op jit(solution)/shard_map/reduce_scatter | solution.py:57
  382.9 99.3 %reduce-scatter.11.cloned.1.call-done = bf16[96,3072]{1,0:T(8,128)(2,1)} async-done(((bf16[768,3072]{1,0:T(8,128)(2,1)}), bf16[96,3072]{1,0:T(8,128)(2,1)}) %reduce-scatter.11.cloned.1.call-update) | async-done | bytes 589840 | tf_op jit(solution)/shard_map/reduce_scatter | solution.py:52
  (15 shorter events, 0.3 us)
Async XLA Ops:
  7.2 85.6 %all-gather.4.cloned.1.call-start = ((), (), s32[]{:S(2)}) async-start(), calls=%async_computation.4 | async-start | bytes 5308416 | tf_op jit(solution)/shard_map/all_gather | solution.py:45
  7.9 39.8 %copy-start = (bf16[128,3072]{1,0:T(8,128)(2,1)S(1)}, bf16[128,3072]{1,0:T(8,128)(2,1)}, u32[]{:S(2)}) copy-start(bf16[128,3072]{1,0:T(8,128)(2,1)} %param.6) | copy-start | bytes 2359300
  7.9 165.1 %all-gather.6.cloned.1.call-start = ((), (), s32[]{:S(2)}) async-start(), calls=%async_computation.5 | async-start | bytes 5308416 | tf_op jit(solution)/shard_map/all_gather | solution.py:47
  8.7 192.6 %all-gather.8.cloned.1.call-start = ((), (), s32[]{:S(2)}) async-start(), calls=%async_computation.7 | async-start | bytes 3932160 | tf_op jit(solution)/shard_map/all_gather | solution.py:46
  8.7 12.3 %collective-permute-start = (bf16[128,3072]{1,0:T(8,128)(2,1)}, bf16[128,3072]{1,0:T(8,128)(2,1)S(1)}, u32[]{:S(2)}, u32[]{:S(2)}) collective-permute-start(bf16[128,3072]{1,0:T(8,128)(2,1)} %param.6), channel_id=1, source_target_pairs={{0,1},{1,2},{2,3},{3,0},{4,5},{5,6},{6,7},{7,4},{8,9},{9,10},{10,1... | collective-permute-start | bytes 2359304 | tf_op jit(solution)/shard_map/ppermute | solution.py:41
  21.0 11.4 %collective-permute-start.1 = (bf16[128,3072]{1,0:T(8,128)(2,1)S(1)}, bf16[128,3072]{1,0:T(8,128)(2,1)S(1)}, u32[]{:S(2)}, u32[]{:S(2)}) collective-permute-start(bf16[128,3072]{1,0:T(8,128)(2,1)S(1)} %collective-permute-done), channel_id=1, source_target_pairs={{0,1},{1,2},{2,3},{3,0},{4,5},{5,6},{6,7},{7,4},{8,9},{9,10},{10,1... | collective-permute-start | bytes 2359304 | tf_op jit(solution)/shard_map/ppermute | solution.py:41
  32.4 12.4 %collective-permute-start.2 = (bf16[128,3072]{1,0:T(8,128)(2,1)S(1)}, bf16[128,3072]{1,0:T(8,128)(2,1)S(1)}, u32[]{:S(2)}, u32[]{:S(2)}) collective-permute-start(bf16[128,3072]{1,0:T(8,128)(2,1)S(1)} %collective-permute-done.1), channel_id=1, source_target_pairs={{0,1},{1,2},{2,3},{3,0},{4,5},{5,6},{6,7},{7,4},{8,9},{9,10},{10,1... | collective-permute-start | bytes 2359304 | tf_op jit(solution)/shard_map/ppermute | solution.py:41
  32.5 209.8 %reduce-scatter.5.cloned.1.call-start = ((), (), s32[]{:S(2)}) async-start(), calls=%async_computation.6 | async-start | bytes 3932160 | tf_op jit(solution)/shard_map/reduce_scatter | solution.py:61
  179.5 103.9 %reduce-scatter.7.cloned.1.call-start = ((), (), s32[]{:S(2)}) async-start(), calls=%async_computation.8 | async-start | bytes 3932160 | tf_op jit(solution)/shard_map/reduce_scatter | solution.py:63
  214.8 168.1 %reduce-scatter.9.cloned.1.call-start = ((), (), s32[]{:S(2)}) async-start(), calls=%async_computation.9 | async-start | bytes 5308416 | tf_op jit(solution)/shard_map/reduce_scatter | solution.py:57
  221.7 260.5 %reduce-scatter.11.cloned.1.call-start = ((), (), s32[]{:S(2)}) async-start(), calls=%async_computation.10 | async-start | bytes 5308416 | tf_op jit(solution)/shard_map/reduce_scatter | solution.py:52
Sparse Core Ops, SparseCore 0:
  10.2 82.5 all-gather.3
  95.0 78.0 all-gather.5
  174.6 26.6 all-gather.7
  204.3 37.9 reduce-scatter.4
  245.4 37.9 reduce-scatter.6
  287.5 95.4 reduce-scatter.8
  387.1 94.9 reduce-scatter.10
